TPU v7x, 32 devices: a whole 2x2x4 slice. The times are simulated.
32 devices in a mesh: groups: 2 (over x), dates: 16 (over z, y, core).
Axes of the slice: x: 2, y: 2, z: 4, core: 2. Of those that a mesh axis runs over, the one named last changes fastest.
Arguments:
- scenes: bfloat16 [64, 16, 7, 256], P(('groups', 'dates')), parts along dimension 0, as said below
- quality: bfloat16 [64, 16, 256], P(('groups', 'dates')), parts along dimension 0, may hold values from 0.099609375 to 1
- pif_mask: float32 [32, 256], P(('groups', 'dates')), parts along dimension 0, may hold values from 0.05 to 1
- counts: int32 [32], P(('groups', 'dates')), parts along dimension 0, may hold values from 1 to 32, as said below
Outputs:
- normalized: bfloat16 [64, 16, 7, 256], P(('groups', 'dates')), parts along dimension 0
There are 2 independent parts, one for each index of `groups`. A program takes and returns all parts, laid end to end along the dimension named above; each array names one. Nothing has to cross between parts.
Inputs may be any that keep to these rules, and one draw needn't show every extreme that they name: Tile t is valid on dates 0 to counts[t] - 1; some tile is valid on all 32 dates. scenes are finite reflectances.
All inputs are finite; a program needn't handle non-finite values.
Results may differ from a plain program's by a relative error of at most 0.0005.
Values may be sent and summed in bfloat16 or wider, within the bound.
A program may use at most 64 MiB of HBM per device.

v0:
```python
import jax
import jax.numpy as jnp
from jax import lax
from jax.sharding import PartitionSpec as P


def solve_fit(weight_sum, sum_x, sum_xx, sum_y, sum_xy):
    total = weight_sum[:, None]
    mean_x = sum_x / total
    mean_y = sum_y / total
    spread = sum_xx / total - mean_x * mean_x + 1e-05
    gain = (sum_xy / total - mean_x * mean_y) / spread
    return (gain, mean_y - gain * mean_x)


def fit_sums_of(weight, values, composite, pif_mask):
    fit = weight * pif_mask[None]
    fitted = fit[:, :, None, :] * values
    weight_sum = jnp.sum(fit, axis=(1, 2))
    sum_x = jnp.sum(fitted, axis=(1, 3))
    sum_xx = jnp.sum(fitted * values, axis=(1, 3))
    sum_y = jnp.sum(fit[:, :, None, :] * composite[None], axis=(1, 3))
    sum_xy = jnp.sum(fitted * composite[None], axis=(1, 3))
    return (weight_sum, sum_x, sum_xx, sum_y, sum_xy)


def local(scenes, quality, pif_mask, counts):
    tile_scenes, tile_quality = (
        lax.all_to_all(scenes, "dates", split_axis=1, concat_axis=0, tiled=True),
        lax.all_to_all(quality, "dates", split_axis=1, concat_axis=0, tiled=True),
    )
    date_ids = jnp.arange(tile_scenes.shape[0], dtype=jnp.int32)
    covered = (date_ids[:, None] < counts[None, :]).astype(jnp.float32)
    weight = tile_quality.astype(jnp.float32) * covered[:, :, None]
    values = tile_scenes.astype(jnp.float32)
    weighted = jnp.sum(weight[:, :, None, :] * values, axis=0)
    totals = jnp.sum(weight, axis=0)
    composite = weighted / totals[:, None, :]
    weight_sum, sum_x, sum_xx, sum_y, sum_xy = fit_sums_of(weight, values, composite, pif_mask)
    sums = (
        lax.psum_scatter(weight_sum, "dates", scatter_dimension=0, tiled=True),
        lax.psum_scatter(sum_x, "dates", scatter_dimension=0, tiled=True),
        lax.psum_scatter(sum_xx, "dates", scatter_dimension=0, tiled=True),
        lax.psum_scatter(sum_y, "dates", scatter_dimension=0, tiled=True),
        lax.psum_scatter(sum_xy, "dates", scatter_dimension=0, tiled=True),
    )
    gain, offset = solve_fit(*sums)
    own_values = scenes.astype(jnp.float32)
    return (gain[:, None, :, None] * own_values + offset[:, None, :, None]).astype(jnp.bfloat16)


def solution(mesh):
    placed = (
        P(("groups", "dates"), None, None, None),
        P(("groups", "dates"), None, None),
        P(("groups", "dates"), None),
        P(("groups", "dates")),
    )
    return jax.shard_map(
        local,
        mesh=mesh,
        in_specs=placed,
        out_specs=P(("groups", "dates"), None, None, None),
        check_vma=False,
    )
```

profile of v0, /device:TPU:0, one launch (start us, length us, event | category | flops | bytes accessed | tf_op | source)
XLA Modules:
  0.0 87.6 jit_solution(16721891539199822126)
XLA Ops:
  0.0 1.3 %copy.29 = bf16[2,16,256]{2,0,1:T(2,128)(2,1)} copy(bf16[2,16,256]{2,1,0:T(8,128)(2,1)} %param.5) | data formatting | bytes 32768 | tf_op args[1]
  1.3 7.4 %all-to-all-start = ((bf16[2,16,256]{2,0,1:T(2,128)(2,1)}), bf16[2,16,256]{2,0,1:T(2,128)(2,1)S(1)}, u32[]{:S(2)}, u32[]{:S(2)}) async-start(bf16[2,16,256]{2,0,1:T(2,128)(2,1)} %copy.29), calls=%async_computation | async-start | bytes 32768 | tf_op jit(solution)/shard_map/all_to_all | solution.py:30
  9.4 1.6 %copy.31 = bf16[2,16,7,256]{3,2,0,1:T(8,128)(2,1)} copy(bf16[2,16,7,256]{3,1,2,0:T(8,128)(2,1)} %param.4) | data formatting | bytes 229376 | tf_op args[0]
  11.0 0.0 copy-start.2
  11.0 0.7 copy-done.2
  11.7 0.6 dynamic-slice
  12.8 2.4 %all-to-all-done = bf16[2,16,256]{2,0,1:T(2,128)(2,1)S(1)} async-done(((bf16[2,16,256]{2,0,1:T(2,128)(2,1)}), bf16[2,16,256]{2,0,1:T(2,128)(2,1)S(1)}, u32[]{:S(2)}, u32[]{:S(2)}) %all-to-all-start) | async-done | bytes 16416 | tf_op jit(solution)/shard_map/all_to_all | solution.py:30
  15.3 3.6 %all-to-all-start.1 = ((bf16[2,16,7,256]{3,2,0,1:T(8,128)(2,1)}), bf16[2,16,7,256]{3,2,0,1:T(8,128)(2,1)S(1)}, u32[]{:S(2)}, u32[]{:S(2)}) async-start(bf16[2,16,7,256]{3,2,0,1:T(8,128)(2,1)} %copy.31), calls=%async_computation.1 | async-start | bytes 262144 | tf_op jit(solution)/shard_map/all_to_all | solution.py:29
  18.9 0.1 reshape.216
  19.0 0.0 copy-start.1
  19.0 0.7 copy-done.1
  19.7 0.1 fusion.7
  19.8 0.5 multiply_reduce_fusion.1
  20.3 0.1 multiply_multiply_fusion.2
  20.3 6.4 %all-to-all-done.1 = bf16[2,16,7,256]{3,2,0,1:T(8,128)(2,1)S(1)} async-done(((bf16[2,16,7,256]{3,2,0,1:T(8,128)(2,1)}), bf16[2,16,7,256]{3,2,0,1:T(8,128)(2,1)S(1)}, u32[]{:S(2)}, u32[]{:S(2)}) %all-to-all-start.1) | async-done | bytes 114720 | tf_op jit(solution)/shard_map/all_to_all | solution.py:29
  26.8 0.1 fusion.6
  26.8 0.2 fusion.2
  27.0 0.0 copy-start
  27.0 0.1 copy.35
  27.1 0.1 copy.40
  27.2 0.1 multiply_reduce_fusion
  27.4 0.1 copy.38
  27.4 0.1 copy.37
  27.5 59.1 %all-reduce.5 = (f32[32,7]{1,0:T(8,128)S(1)}, f32[32,7]{1,0:T(8,128)S(1)}, f32[32]{0:T(128)S(1)}, f32[32,7]{1,0:T(8,128)S(1)}, f32[32,7]{1,0:T(8,128)S(1)}) all-reduce(f32[32,7]{1,0:T(8,128)S(1)} %bitcast.57, f32[32,7]{1,0:T(8,128)S(1)} %bitcast.58, ...), channel_id=2, replica_groups=mesh['groups'=2,'dates'=16] {'dates'}, use_global_device_ids=true, to_apply=%region_3.0.clone | all-reduce | flops 928 | bytes 7424
  86.7 0.1 dynamic-slice.3
  86.7 0.1 multiply_subtract_fusion
  86.8 0.0 copy-done
  86.8 0.8 add_convert_fusion
  (7 shorter events, 0.1 us)
Async XLA Ops:
  1.3 13.9 %all-to-all-start = ((bf16[2,16,256]{2,0,1:T(2,128)(2,1)}), bf16[2,16,256]{2,0,1:T(2,128)(2,1)S(1)}, u32[]{:S(2)}, u32[]{:S(2)}) async-start(bf16[2,16,256]{2,0,1:T(2,128)(2,1)} %copy.29), calls=%async_computation | async-start | bytes 32768 | tf_op jit(solution)/shard_map/all_to_all | solution.py:30
  11.0 0.7 copy-start.2
  15.3 11.5 %all-to-all-start.1 = ((bf16[2,16,7,256]{3,2,0,1:T(8,128)(2,1)}), bf16[2,16,7,256]{3,2,0,1:T(8,128)(2,1)S(1)}, u32[]{:S(2)}, u32[]{:S(2)}) async-start(bf16[2,16,7,256]{3,2,0,1:T(8,128)(2,1)} %copy.31), calls=%async_computation.1 | async-start | bytes 262144 | tf_op jit(solution)/shard_map/all_to_all | solution.py:29
  19.0 0.7 copy-start.1
  27.0 59.8 %copy-start = (bf16[2,16,7,256]{3,1,2,0:T(8,128)(2,1)S(1)}, bf16[2,16,7,256]{3,1,2,0:T(8,128)(2,1)}, u32[]{:S(2)}) copy-start(bf16[2,16,7,256]{3,1,2,0:T(8,128)(2,1)} %param.4) | copy-start | bytes 344068
where the time goes:
time: 88 us; the launch traced here: 87.6 us
  blocking collectives  59.1 us (67%)
  starting transfers between devices  11 us (12%)
  waiting for transfers between devices  8.86 us (10%)
  local copies, waits for them, and re-layouts  5.36 us (6%)
  other arithmetic  1.88 us (2%)
  between operations  1.35 us (2%)
    unnamed x1, blocking collectives  59.1 us
    all_to_all x1, starting transfers between devices, local(): lax.all_to_all(quality, 'dates', split_axis=1, concat_axis=0, tiled=True)  7.41 us
    all_to_all x1, waiting for transfers between devices, local(): lax.all_to_all(scenes, 'dates', split_axis=1, concat_axis=0, tiled=True)  6.41 us
    unnamed x10, local copies, waits for them, and re-layouts  4.9 us
    all_to_all x1, starting transfers between devices, local(): lax.all_to_all(scenes, 'dates', split_axis=1, concat_axis=0, tiled=True)  3.59 us
    all_to_all x1, waiting for transfers between devices, local(): lax.all_to_all(quality, 'dates', split_axis=1, concat_axis=0, tiled=True)  2.44 us
  transfers between devices with their start and end apart: 2, of which 2 were waited for; matrix products, arithmetic and copies ran while one was open for 3% of the time, Pallas kernels for 0%

commit v1 on v0

v1 whole, which is shorter than its diff:
```python
import functools

import jax
import jax.numpy as jnp
from jax import lax
from jax.experimental import pallas as pl
from jax.experimental.pallas import tpu as pltpu
from jax.sharding import PartitionSpec as P

AXIS = "dates"
LANES = 128


def fused(n, scenes_hbm, quality_hbm, mask_hbm, counts_ref, out_ref,
          own, own_q, q_rows, mask, stage, recv, fitted, part, got,
          local_sem, send_a, recv_a, send_b, recv_b):
    dates, tiles, bands, pix = own.shape
    mine = tiles // n
    rows = bands + 1
    me = lax.axis_index(AXIS)

    barrier = pltpu.get_barrier_semaphore()

    def greet(k, carry):
        pl.semaphore_signal(barrier, inc=1, device_id={AXIS: lax.rem(me + k, n)})
        return carry

    lax.fori_loop(1, n, greet, 0)
    loads = [
        pltpu.make_async_copy(quality_hbm, own_q, local_sem.at[0]),
        pltpu.make_async_copy(scenes_hbm, own, local_sem.at[1]),
        pltpu.make_async_copy(mask_hbm, mask, local_sem.at[2]),
    ]
    for load in loads:
        load.start()
    for load in loads:
        load.wait()

    q_rows[...] = own_q[...].astype(jnp.float32)

    def stage_tile(t, carry):
        for i in range(dates):
            block = jnp.concatenate(
                [own[i, t].astype(jnp.float32), q_rows[i, pl.ds(t, 1), :]], axis=0
            )
            stage[t, i] = block.astype(jnp.bfloat16)
        return carry

    lax.fori_loop(0, tiles, stage_tile, 0, unroll=min(tiles, 16))
    recv[me] = stage[pl.ds(me * mine, mine)]

    pl.semaphore_wait(barrier, n - 1)

    def block_copy(k):
        peer = lax.rem(me + k, n)
        return pltpu.make_async_remote_copy(
            src_ref=stage.at[pl.ds(peer * mine, mine)],
            dst_ref=recv.at[me],
            send_sem=send_a.at[peer],
            recv_sem=recv_a.at[me],
            device_id={AXIS: peer},
        )

    def block_arrival(source):
        return pltpu.make_async_remote_copy(
            src_ref=stage.at[pl.ds(source * mine, mine)],
            dst_ref=recv.at[source],
            send_sem=send_a.at[source],
            recv_sem=recv_a.at[source],
            device_id={AXIS: source},
        )

    def send_block(k, carry):
        block_copy(k).start()
        return carry

    lax.fori_loop(1, n, send_block, 0)

    last_row = lax.broadcasted_iota(jnp.int32, (rows, pix), 0) == bands
    lane = lax.broadcasted_iota(jnp.int32, (rows, LANES), 1)

    def lane_sum(values):
        return jnp.sum(values, axis=1, keepdims=True)

    def take(source, totals):
        totals = list(totals)
        sums = jnp.zeros((rows, LANES), jnp.float32)
        for i in range(dates):
            sum_x = sum_xx = 0.0
            for t in range(mine):
                block = recv[source, t, i].astype(jnp.float32)
                covered = jnp.where(source * dates + i < counts_ref[t], 1.0, 0.0)
                weight = block[bands:] * covered
                values = jnp.where(last_row, 1.0, block)
                weighted = weight * values
                totals[t] = totals[t] + weighted
                fit_x = weighted * mask[t:t + 1, :]
                fitted[source, t, i] = fit_x
                sum_x = sum_x + fit_x
                sum_xx = sum_xx + fit_x * values
            sums = jnp.where(lane == 4 * i, lane_sum(sum_x), sums)
            sums = jnp.where(lane == 4 * i + 1, lane_sum(sum_xx), sums)
        part[source] = sums
        return tuple(totals)

    totals = tuple(jnp.zeros((rows, pix), jnp.float32) for _ in range(mine))
    totals = take(me, totals)

    def take_arrival(k, totals):
        source = lax.rem(me - k + n, n)
        block_arrival(source).wait_recv()
        return take(source, totals)

    totals = lax.fori_loop(1, n, take_arrival, totals)
    composite = [total / total[bands:] for total in totals]

    def finish(source):
        sums = part[source]
        for i in range(dates):
            sum_y = sum_xy = 0.0
            for t in range(mine):
                fit_x = fitted[source, t, i]
                sum_y = sum_y + fit_x[bands:] * composite[t]
                sum_xy = sum_xy + fit_x * composite[t]
            sums = jnp.where(lane == 4 * i + 2, lane_sum(sum_y), sums)
            sums = jnp.where(lane == 4 * i + 3, lane_sum(sum_xy), sums)
        part[source] = sums

    def finish_peer(k, carry):
        finish(lax.rem(me + k, n))
        return carry

    lax.fori_loop(0, n, finish_peer, 0, unroll=min(n, 16))
    got[me] = part[me]

    def sums_copy(k):
        peer = lax.rem(me + k, n)
        return pltpu.make_async_remote_copy(
            src_ref=part.at[peer],
            dst_ref=got.at[me],
            send_sem=send_b.at[peer],
            recv_sem=recv_b.at[me],
            device_id={AXIS: peer},
        )

    def send_sums(k, carry):
        sums_copy(k).start()
        return carry

    lax.fori_loop(1, n, send_sums, 0)

    def take_sums(k, total):
        source = lax.rem(me - k + n, n)
        pltpu.make_async_remote_copy(
            src_ref=part.at[source],
            dst_ref=got.at[source],
            send_sem=send_b.at[source],
            recv_sem=recv_b.at[source],
            device_id={AXIS: source},
        ).wait_recv()
        return total + got[source]

    sums = lax.fori_loop(1, n, take_sums, got[me])
    lines = []
    for i in range(dates):
        sum_x, sum_xx, sum_y, sum_xy = (sums[:, 4 * i + s:4 * i + s + 1] for s in range(4))
        total = sum_x[bands:]
        mean_x = sum_x / total
        mean_y = sum_y / total
        spread = sum_xx / total - mean_x * mean_x + 1e-5
        gain = (sum_xy / total - mean_x * mean_y) / spread
        offset = mean_y - gain * mean_x
        lines.append((
            jnp.broadcast_to(gain[:bands], (bands, pix)),
            jnp.broadcast_to(offset[:bands], (bands, pix)),
        ))

    def apply(t, carry):
        for i in range(dates):
            gain, offset = lines[i]
            out_ref[i, t] = (gain * own[i, t].astype(jnp.float32) + offset).astype(out_ref.dtype)
        return carry

    lax.fori_loop(0, tiles, apply, 0, unroll=min(tiles, 16))

    def drain(k, carry):
        block_copy(k).wait_send()
        sums_copy(k).wait_send()
        return carry

    lax.fori_loop(1, n, drain, 0)


def local(n, scenes, quality, pif_mask, counts):
    dates, tiles, bands, pix = scenes.shape
    mine = tiles // n
    rows = bands + 1
    anywhere = pl.BlockSpec(memory_space=pl.ANY)
    return pl.pallas_call(
        functools.partial(fused, n),
        out_shape=jax.ShapeDtypeStruct(scenes.shape, scenes.dtype),
        in_specs=[anywhere, anywhere, anywhere, pl.BlockSpec(memory_space=pltpu.SMEM)],
        out_specs=pl.BlockSpec(memory_space=pltpu.VMEM),
        scratch_shapes=[
            pltpu.VMEM(scenes.shape, scenes.dtype),
            pltpu.VMEM(quality.shape, quality.dtype),
            pltpu.VMEM(quality.shape, jnp.float32),
            pltpu.VMEM(pif_mask.shape, jnp.float32),
            pltpu.VMEM((tiles, dates, rows, pix), scenes.dtype),
            pltpu.VMEM((n, mine, dates, rows, pix), scenes.dtype),
            pltpu.VMEM((n, mine, dates, rows, pix), jnp.float32),
            pltpu.VMEM((n, rows, LANES), jnp.float32),
            pltpu.VMEM((n, rows, LANES), jnp.float32),
            pltpu.SemaphoreType.DMA((3,)),
            pltpu.SemaphoreType.DMA((n,)),
            pltpu.SemaphoreType.DMA((n,)),
            pltpu.SemaphoreType.DMA((n,)),
            pltpu.SemaphoreType.DMA((n,)),
        ],
        compiler_params=pltpu.CompilerParams(collective_id=0, has_side_effects=True),
    )(scenes, quality, pif_mask, counts)


def solution(mesh):
    both = ("groups", AXIS)
    placed = (P(both, None, None, None), P(both, None, None), P(both, None), P(both))
    return jax.shard_map(
        functools.partial(local, mesh.shape[AXIS]),
        mesh=mesh,
        in_specs=placed,
        out_specs=placed[0],
        check_vma=False,
    )
```

time: 88 us -> 21.6 us (0.25)
  blocking collectives: 59.1 us -> 0 us
  Pallas kernels: 0 us -> 17.6 us
  starting transfers between devices: 11 us -> 0 us
  waiting for transfers between devices: 8.86 us -> 0 us
  local copies, waits for them, and re-layouts: 5.36 us -> 3.16 us
  other arithmetic: 1.88 us -> 0 us
    unnamed x1 -> x0, blocking collectives: 59.1 us -> none
    pallas_call x0 -> x1, Pallas kernels: none -> 17.6 us  [local(): pl.pallas_call(functools.partial(fused, n), out_shape=jax.ShapeDtypeStruc...]
    all_to_all x2 -> x0, starting transfers between devices: 11 us -> none  [the longest x1 7.41 us: local(): lax.all_to_all(quality, 'dates', split_axis=1, concat_axis=0, tiled=True)]
    all_to_all x2 -> x0, waiting for transfers between devices: 8.86 us -> none  [the longest x1 6.41 us: local(): lax.all_to_all(scenes, 'dates', split_axis=1, concat_axis=0, tiled=True)]
    unnamed x10 -> x1, local copies, waits for them, and re-layouts: 4.9 us -> 1.58 us
    pallas_call x0 -> x1, local copies, waits for them, and re-layouts: none -> 1.57 us  [local(): pl.pallas_call(functools.partial(fused, n), out_shape=jax.ShapeDtypeStruc...]
  transfers between devices with their start and end apart: 2 -> 0, of which waited for: 2 -> 0; matrix products, arithmetic and copies ran while one was open for 3% -> 0% of each run, Pallas kernels for 0% -> 0%
where the time goes in v1:
time: 21.6 us; the launch traced here: 21.4 us
  Pallas kernels  17.6 us (81%)
  local copies, waits for them, and re-layouts  3.16 us (15%)
  between operations  0.66 us (3%)
    pallas_call x1, Pallas kernels, local(): pl.pallas_call(functools.partial(fused, n), out_shape=jax.ShapeDtypeStruc...  17.6 us
    unnamed x1, local copies, waits for them, and re-layouts  1.58 us
    pallas_call x1, local copies, waits for them, and re-layouts, local(): pl.pallas_call(functools.partial(fused, n), out_shape=jax.ShapeDtypeStruc...  1.57 us

profile of v1, /device:TPU:0, one launch (start us, length us, event | category | flops | bytes accessed | tf_op | source)
XLA Modules:
  0.0 21.4 jit_solution(10248627839376571357)
XLA Ops:
  0.7 1.6 %copy.5.scenes_hbm = bf16[2,16,7,256]{3,2,1,0:T(8,128)(2,1)} copy(bf16[2,16,7,256]{3,1,2,0:T(8,128)(2,1)} %param.4) | data formatting | bytes 229376 | tf_op args[0]
  2.2 17.6 %shard_map.46 = bf16[2,16,7,256]{3,2,1,0:T(8,128)(2,1)} custom-call(bf16[2,16,7,256]{3,2,1,0:T(8,128)(2,1)} %copy.5.scenes_hbm, bf16[2,16,256]{2,1,0:T(8,128)(2,1)} %quality_hbm.1, f32[1,256]{1,0:T(1,128)} %mask_hbm.1, s32[1]{0:T(128)S(6)} %copy.7.counts_ref), custom_call_target="tpu_custom_call" | custom-call | tf_op jit(solution)/shard_map/pallas_call | solution.py:199
  19.8 1.6 %copy.6 = bf16[2,16,7,256]{3,1,2,0:T(8,128)(2,1)} copy(bf16[2,16,7,256]{3,2,1,0:T(8,128)(2,1)} %shard_map.46) | data formatting | bytes 229376 | tf_op jit(solution)/shard_map/pallas_call | solution.py:199

commit v2 on v1

--- a/solution.py
+++ b/solution.py
@@ -12,11 +12,11 @@
 
 
 def fused(n, scenes_hbm, quality_hbm, mask_hbm, counts_ref, out_ref,
-          own, own_q, q_rows, mask, stage, recv, fitted, part, got,
+          own, own_q, wide, mask, stage, recv, fitted, part, got,
           local_sem, send_a, recv_a, send_b, recv_b):
-    dates, tiles, bands, pix = own.shape
+    dates, bands, tiles, pix = own.shape
     mine = tiles // n
-    rows = bands + 1
+    rows, halves = bands + 1, pix // LANES
     me = lax.axis_index(AXIS)
 
     barrier = pltpu.get_barrier_semaphore()
@@ -36,14 +36,18 @@
     for load in loads:
         load.wait()
 
-    q_rows[...] = own_q[...].astype(jnp.float32)
+    for i in range(dates):
+        for h in range(halves):
+            columns = slice(h * LANES, (h + 1) * LANES)
+            for b in range(bands):
+                wide[i, h, b * tiles:(b + 1) * tiles] = own[i, b, :, columns].astype(jnp.float32)
+            wide[i, h, bands * tiles:] = own_q[i, :, columns].astype(jnp.float32)
 
     def stage_tile(t, carry):
         for i in range(dates):
-            block = jnp.concatenate(
-                [own[i, t].astype(jnp.float32), q_rows[i, pl.ds(t, 1), :]], axis=0
-            )
-            stage[t, i] = block.astype(jnp.bfloat16)
+            for h in range(halves):
+                block = wide[i, h, pl.ds(t, rows, stride=tiles), :]
+                stage[t, i, :, h * LANES:(h + 1) * LANES] = block.astype(jnp.bfloat16)
         return carry
 
     lax.fori_loop(0, tiles, stage_tile, 0, unroll=min(tiles, 16))
@@ -161,7 +165,6 @@
         return total + got[source]
 
     sums = lax.fori_loop(1, n, take_sums, got[me])
-    lines = []
     for i in range(dates):
         sum_x, sum_xx, sum_y, sum_xy = (sums[:, 4 * i + s:4 * i + s + 1] for s in range(4))
         total = sum_x[bands:]
@@ -170,18 +173,13 @@
         spread = sum_xx / total - mean_x * mean_x + 1e-5
         gain = (sum_xy / total - mean_x * mean_y) / spread
         offset = mean_y - gain * mean_x
-        lines.append((
-            jnp.broadcast_to(gain[:bands], (bands, pix)),
-            jnp.broadcast_to(offset[:bands], (bands, pix)),
-        ))
-
-    def apply(t, carry):
-        for i in range(dates):
-            gain, offset = lines[i]
-            out_ref[i, t] = (gain * own[i, t].astype(jnp.float32) + offset).astype(out_ref.dtype)
-        return carry
-
-    lax.fori_loop(0, tiles, apply, 0, unroll=min(tiles, 16))
+        gain = jnp.broadcast_to(gain, (rows, LANES))
+        offset = jnp.broadcast_to(offset, (rows, LANES))
+        for b in range(bands):
+            for h in range(halves):
+                values = wide[i, h, b * tiles:(b + 1) * tiles]
+                scaled = gain[b:b + 1] * values + offset[b:b + 1]
+                out_ref[i, b, :, h * LANES:(h + 1) * LANES] = scaled.astype(out_ref.dtype)
 
     def drain(k, carry):
         block_copy(k).wait_send()
@@ -192,11 +190,12 @@
 
 
 def local(n, scenes, quality, pif_mask, counts):
-    dates, tiles, bands, pix = scenes.shape
+    scenes = scenes.transpose(0, 2, 1, 3)
+    dates, bands, tiles, pix = scenes.shape
     mine = tiles // n
     rows = bands + 1
     anywhere = pl.BlockSpec(memory_space=pl.ANY)
-    return pl.pallas_call(
+    out = pl.pallas_call(
         functools.partial(fused, n),
         out_shape=jax.ShapeDtypeStruct(scenes.shape, scenes.dtype),
         in_specs=[anywhere, anywhere, anywhere, pl.BlockSpec(memory_space=pltpu.SMEM)],
@@ -204,7 +203,7 @@
         scratch_shapes=[
             pltpu.VMEM(scenes.shape, scenes.dtype),
             pltpu.VMEM(quality.shape, quality.dtype),
-            pltpu.VMEM(quality.shape, jnp.float32),
+            pltpu.VMEM((dates, pix // LANES, rows * tiles, LANES), jnp.float32),
             pltpu.VMEM(pif_mask.shape, jnp.float32),
             pltpu.VMEM((tiles, dates, rows, pix), scenes.dtype),
             pltpu.VMEM((n, mine, dates, rows, pix), scenes.dtype),
@@ -219,6 +218,7 @@
         ],
         compiler_params=pltpu.CompilerParams(collective_id=0, has_side_effects=True),
     )(scenes, quality, pif_mask, counts)
+    return out.transpose(0, 2, 1, 3)
 
 
 def solution(mesh):

time: 21.6 us -> 20.1 us (0.931)
  local copies, waits for them, and re-layouts: 3.16 us -> 1.55 us
    pallas_call x1 -> x0, local copies, waits for them, and re-layouts: 1.57 us -> none  [local(): pl.pallas_call(functools.partial(fused, n), out_shape=jax.ShapeDtypeStruc...]
where the time goes in v2:
time: 20.1 us; the launch traced here: 19.9 us
  Pallas kernels  17.7 us (88%)
  local copies, waits for them, and re-layouts  1.55 us (8%)
  between operations  0.66 us (3%)
    pallas_call x1, Pallas kernels, local(): pl.pallas_call(functools.partial(fused, n), out_shape=jax.ShapeDtypeStruc...  17.7 us
    unnamed x1, local copies, waits for them, and re-layouts  1.55 us

profile of v2, /device:TPU:0, one launch (start us, length us, event | category | flops | bytes accessed | tf_op | source)
XLA Modules:
  0.0 19.9 jit_solution(5141957736392483232)
XLA Ops:
  0.7 17.7 %shard_map.46 = bf16[2,7,16,256]{3,2,1,0:T(8,128)(2,1)} custom-call(bf16[2,7,16,256]{3,2,1,0:T(8,128)(2,1)} %bitcast.3, bf16[2,16,256]{2,1,0:T(8,128)(2,1)} %quality_hbm.1, f32[1,256]{1,0:T(1,128)} %mask_hbm.1, s32[1]{0:T(128)S(6)} %copy.6.counts_ref), custom_call_target="tpu_custom_call" | custom-call | tf_op jit(solution)/shard_map/pallas_call | solution.py:198
  18.3 1.6 %copy.7 = bf16[2,16,7,256]{3,1,2,0:T(8,128)(2,1)} copy(bf16[2,16,7,256]{3,1,2,0:T(8,128)(2,1)} %bitcast.2) | data formatting | bytes 229376

commit v3 on v2

--- a/solution.py
+++ b/solution.py
@@ -11,8 +11,8 @@
 LANES = 128
 
 
-def fused(n, scenes_hbm, quality_hbm, mask_hbm, counts_ref, out_ref,
-          own, own_q, wide, mask, stage, recv, fitted, part, got,
+def fused(n, scenes_hbm, quality_hbm, mask_hbm, counts_hbm, out_ref,
+          own, own_q, wide, mask, counts_ref, stage, recv, fitted, part, got,
           local_sem, send_a, recv_a, send_b, recv_b):
     dates, bands, tiles, pix = own.shape
     mine = tiles // n
@@ -30,6 +30,7 @@
         pltpu.make_async_copy(quality_hbm, own_q, local_sem.at[0]),
         pltpu.make_async_copy(scenes_hbm, own, local_sem.at[1]),
         pltpu.make_async_copy(mask_hbm, mask, local_sem.at[2]),
+        pltpu.make_async_copy(counts_hbm, counts_ref, local_sem.at[3]),
     ]
     for load in loads:
         load.start()
@@ -194,29 +195,32 @@
     dates, bands, tiles, pix = scenes.shape
     mine = tiles // n
     rows = bands + 1
-    anywhere = pl.BlockSpec(memory_space=pl.ANY)
+    in_place = pl.BlockSpec(memory_space=pltpu.HBM)
     out = pl.pallas_call(
         functools.partial(fused, n),
         out_shape=jax.ShapeDtypeStruct(scenes.shape, scenes.dtype),
-        in_specs=[anywhere, anywhere, anywhere, pl.BlockSpec(memory_space=pltpu.SMEM)],
+        in_specs=[in_place] * 4,
         out_specs=pl.BlockSpec(memory_space=pltpu.VMEM),
         scratch_shapes=[
             pltpu.VMEM(scenes.shape, scenes.dtype),
             pltpu.VMEM(quality.shape, quality.dtype),
             pltpu.VMEM((dates, pix // LANES, rows * tiles, LANES), jnp.float32),
             pltpu.VMEM(pif_mask.shape, jnp.float32),
+            pltpu.SMEM(counts.shape, jnp.int32),
             pltpu.VMEM((tiles, dates, rows, pix), scenes.dtype),
             pltpu.VMEM((n, mine, dates, rows, pix), scenes.dtype),
             pltpu.VMEM((n, mine, dates, rows, pix), jnp.float32),
             pltpu.VMEM((n, rows, LANES), jnp.float32),
             pltpu.VMEM((n, rows, LANES), jnp.float32),
-            pltpu.SemaphoreType.DMA((3,)),
+            pltpu.SemaphoreType.DMA((4,)),
             pltpu.SemaphoreType.DMA((n,)),
             pltpu.SemaphoreType.DMA((n,)),
             pltpu.SemaphoreType.DMA((n,)),
             pltpu.SemaphoreType.DMA((n,)),
         ],
-        compiler_params=pltpu.CompilerParams(collective_id=0, has_side_effects=True),
+        compiler_params=pltpu.CompilerParams(
+            collective_id=0, has_side_effects=True, vmem_limit_bytes=32 * 2**20
+        ),
     )(scenes, quality, pif_mask, counts)
     return out.transpose(0, 2, 1, 3)
 

time: 20.1 us -> 20.8 us (1.035)
  local copies, waits for them, and re-layouts: 1.55 us -> 2.94 us
  Pallas kernels: 17.7 us -> 17 us
    unnamed x1 -> x7, local copies, waits for them, and re-layouts: 1.55 us -> 2.94 us
    pallas_call x1, Pallas kernels: 17.7 us -> 17 us  [local(): pl.pallas_call(functools.partial(fused, n), out_shape=jax.ShapeDtypeStruc...]
where the time goes in v3:
time: 20.8 us; the launch traced here: 20.6 us
  Pallas kernels  17 us (82%)
  local copies, waits for them, and re-layouts  2.94 us (14%)
  between operations  0.67 us (3%)
    pallas_call x1, Pallas kernels, local(): pl.pallas_call(functools.partial(fused, n), out_shape=jax.ShapeDtypeStruc...  17 us
    unnamed x7, local copies, waits for them, and re-layouts  2.94 us

profile of v3, /device:TPU:0, one launch (start us, length us, event | category | flops | bytes accessed | tf_op | source)
XLA Modules:
  0.0 20.6 jit_solution(390631831491760783)
XLA Ops:
  0.7 0.0 copy-start.2
  0.7 0.7 %copy-done.2 = f32[1,256]{1,0:T(1,128)S(1)} copy-done((f32[1,256]{1,0:T(1,128)S(1)}, f32[1,256]{1,0:T(1,128)}, u32[]{:S(2)}) %copy-start.2) | copy-done | bytes 1048
  1.3 0.0 copy-start
  1.3 0.9 %copy-done = bf16[2,16,7,256]{3,1,2,0:T(8,128)(2,1)S(1)} copy-done((bf16[2,16,7,256]{3,1,2,0:T(8,128)(2,1)S(1)}, bf16[2,16,7,256]{3,1,2,0:T(8,128)(2,1)}, u32[]{:S(2)}) %copy-start) | copy-done | bytes 114712
  2.2 0.0 copy-start.1
  2.2 0.7 %copy-done.1 = bf16[2,16,256]{2,1,0:T(8,128)(2,1)S(1)} copy-done((bf16[2,16,256]{2,1,0:T(8,128)(2,1)S(1)}, bf16[2,16,256]{2,1,0:T(8,128)(2,1)}, u32[]{:S(2)}) %copy-start.1) | copy-done | bytes 16408
  2.9 17.0 %shard_map.46 = bf16[2,7,16,256]{3,2,1,0:T(8,128)(2,1)S(1)} custom-call(bf16[2,7,16,256]{3,2,1,0:T(8,128)(2,1)S(1)} %bitcast.3, bf16[2,16,256]{2,1,0:T(8,128)(2,1)S(1)} %copy-done.1, f32[1,256]{1,0:T(1,128)S(1)} %copy-done.2, s32[1]{0:T(128)S(6)} %copy.6.counts_hbm), custom_call_target="tpu_custom_call" | custom-call | tf_op jit(solution)/shard_map/pallas_call | solution.py:199
  19.9 0.6 %copy.7 = bf16[2,16,7,256]{3,1,2,0:T(8,128)(2,1)} copy(bf16[2,16,7,256]{3,1,2,0:T(8,128)(2,1)S(1)} %bitcast.2) | data formatting | bytes 229376
Async XLA Ops:
  0.7 0.7 %copy-start.2 = (f32[1,256]{1,0:T(1,128)S(1)}, f32[1,256]{1,0:T(1,128)}, u32[]{:S(2)}) copy-start(f32[1,256]{1,0:T(1,128)} %mask_hbm.1) | copy-start | bytes 3076
  1.3 0.9 %copy-start = (bf16[2,16,7,256]{3,1,2,0:T(8,128)(2,1)S(1)}, bf16[2,16,7,256]{3,1,2,0:T(8,128)(2,1)}, u32[]{:S(2)}) copy-start(bf16[2,16,7,256]{3,1,2,0:T(8,128)(2,1)} %param.4) | copy-start | bytes 344068
  2.2 0.7 %copy-start.1 = (bf16[2,16,256]{2,1,0:T(8,128)(2,1)S(1)}, bf16[2,16,256]{2,1,0:T(8,128)(2,1)}, u32[]{:S(2)}) copy-start(bf16[2,16,256]{2,1,0:T(8,128)(2,1)} %quality_hbm.1) | copy-start | bytes 49156

commit v4 on v2

--- a/solution.py
+++ b/solution.py
@@ -194,11 +194,11 @@
     dates, bands, tiles, pix = scenes.shape
     mine = tiles // n
     rows = bands + 1
-    anywhere = pl.BlockSpec(memory_space=pl.ANY)
+    in_place = pl.BlockSpec(memory_space=pltpu.HBM)
     out = pl.pallas_call(
         functools.partial(fused, n),
         out_shape=jax.ShapeDtypeStruct(scenes.shape, scenes.dtype),
-        in_specs=[anywhere, anywhere, anywhere, pl.BlockSpec(memory_space=pltpu.SMEM)],
+        in_specs=[in_place] * 3 + [pl.BlockSpec(memory_space=pltpu.SMEM)],
         out_specs=pl.BlockSpec(memory_space=pltpu.VMEM),
         scratch_shapes=[
             pltpu.VMEM(scenes.shape, scenes.dtype),
@@ -216,8 +216,10 @@
             pltpu.SemaphoreType.DMA((n,)),
             pltpu.SemaphoreType.DMA((n,)),
         ],
-        compiler_params=pltpu.CompilerParams(collective_id=0, has_side_effects=True),
-    )(scenes, quality, pif_mask, counts)
+        compiler_params=pltpu.CompilerParams(
+            collective_id=0, has_side_effects=True, vmem_limit_bytes=32 * 2**20
+        ),
+    )(*(pltpu.with_memory_space_constraint(a, pltpu.HBM) for a in (scenes, quality, pif_mask)), counts)
     return out.transpose(0, 2, 1, 3)
 
 

time: 20.1 us -> 18.6 us (0.925)
  local copies, waits for them, and re-layouts: 1.55 us -> 0.65 us
  Pallas kernels: 17.7 us -> 17 us
    unnamed x1, local copies, waits for them, and re-layouts: 1.55 us -> 0.65 us
    pallas_call x1, Pallas kernels: 17.7 us -> 17 us  [local(): pl.pallas_call(functools.partial(fused, n), out_shape=jax.ShapeDtypeStruc...]
where the time goes in v4:
time: 18.6 us; the launch traced here: 18.3 us
  Pallas kernels  17 us (91%)
  between operations  0.66 us (4%)
  local copies, waits for them, and re-layouts  0.65 us (3%)
    pallas_call x1, Pallas kernels, local(): pl.pallas_call(functools.partial(fused, n), out_shape=jax.ShapeDtypeStruc...  17 us
    unnamed x1, local copies, waits for them, and re-layouts  0.65 us

profile of v4, /device:TPU:0, one launch (start us, length us, event | category | flops | bytes accessed | tf_op | source)
XLA Modules:
  0.0 18.3 jit_solution(10240495823925091924)
XLA Ops:
  0.7 17.0 %shard_map.46 = bf16[2,7,16,256]{3,2,1,0:T(8,128)(2,1)S(1)} custom-call(bf16[2,7,16,256]{3,2,1,0:T(8,128)(2,1)} %bitcast.3, bf16[2,16,256]{2,1,0:T(8,128)(2,1)} %quality_hbm.1, f32[1,256]{1,0:T(1,128)} %mask_hbm.1, s32[1]{0:T(128)S(6)} %copy.6.counts_ref), custom_call_target="tpu_custom_call" | custom-call | tf_op jit(solution)/shard_map/pallas_call | solution.py:198
  17.7 0.6 %copy.7 = bf16[2,16,7,256]{3,1,2,0:T(8,128)(2,1)} copy(bf16[2,16,7,256]{3,1,2,0:T(8,128)(2,1)S(1)} %bitcast.2) | data formatting | bytes 229376

commit v5 on v4

--- a/solution.py
+++ b/solution.py
@@ -12,7 +12,7 @@
 
 
 def fused(n, scenes_hbm, quality_hbm, mask_hbm, counts_ref, out_ref,
-          own, own_q, wide, mask, stage, recv, fitted, part, got,
+          own, own_q, wide, mask, stage, recv, fitted, early, part, got,
           local_sem, send_a, recv_a, send_b, recv_b):
     dates, bands, tiles, pix = own.shape
     mine = tiles // n
@@ -55,8 +55,13 @@
 
     pl.semaphore_wait(barrier, n - 1)
 
-    def block_copy(k):
-        peer = lax.rem(me + k, n)
+    def peer_at(spot):
+        step = spot - 1
+        half, odd = lax.div(step, 2), lax.rem(step, 2)
+        ahead = (1 + half) * (1 - odd) + (n - 1 - half) * odd
+        return lax.rem(me + ahead, n)
+
+    def block_copy(peer):
         return pltpu.make_async_remote_copy(
             src_ref=stage.at[pl.ds(peer * mine, mine)],
             dst_ref=recv.at[me],
@@ -75,7 +80,7 @@
         )
 
     def send_block(k, carry):
-        block_copy(k).start()
+        block_copy(peer_at(n - k)).start()
         return carry
 
     lax.fori_loop(1, n, send_block, 0)
@@ -86,40 +91,52 @@
     def lane_sum(values):
         return jnp.sum(values, axis=1, keepdims=True)
 
-    def take(source, totals):
+    def take(sources, totals):
         totals = list(totals)
-        sums = jnp.zeros((rows, LANES), jnp.float32)
-        for i in range(dates):
-            sum_x = sum_xx = 0.0
-            for t in range(mine):
-                block = recv[source, t, i].astype(jnp.float32)
-                covered = jnp.where(source * dates + i < counts_ref[t], 1.0, 0.0)
-                weight = block[bands:] * covered
-                values = jnp.where(last_row, 1.0, block)
-                weighted = weight * values
-                totals[t] = totals[t] + weighted
-                fit_x = weighted * mask[t:t + 1, :]
+        kept = []
+        for source in sources:
+            sums = jnp.zeros((rows, LANES), jnp.float32)
+            parts = []
+            for i in range(dates):
+                sum_x = sum_xx = 0.0
+                for t in range(mine):
+                    block = recv[source, t, i].astype(jnp.float32)
+                    covered = jnp.where(source * dates + i < counts_ref[t], 1.0, 0.0)
+                    weight = block[bands:] * covered
+                    values = jnp.where(last_row, 1.0, block)
+                    weighted = weight * values
+                    totals[t] = totals[t] + weighted
+                    fit_x = weighted * mask[t:t + 1, :]
+                    parts.append((t, i, fit_x))
+                    sum_x = sum_x + fit_x
+                    sum_xx = sum_xx + fit_x * values
+                sums = jnp.where(lane == 4 * i, lane_sum(sum_x), sums)
+                sums = jnp.where(lane == 4 * i + 1, lane_sum(sum_xx), sums)
+            kept.append((source, sums, parts))
+        for source, sums, parts in kept:
+            early[source] = sums
+            for t, i, fit_x in parts:
                 fitted[source, t, i] = fit_x
-                sum_x = sum_x + fit_x
-                sum_xx = sum_xx + fit_x * values
-            sums = jnp.where(lane == 4 * i, lane_sum(sum_x), sums)
-            sums = jnp.where(lane == 4 * i + 1, lane_sum(sum_xx), sums)
-        part[source] = sums
         return tuple(totals)
 
+    batch = 4 if n % 4 == 0 else 1
     totals = tuple(jnp.zeros((rows, pix), jnp.float32) for _ in range(mine))
-    totals = take(me, totals)
-
-    def take_arrival(k, totals):
-        source = lax.rem(me - k + n, n)
+    first = [peer_at(spot) for spot in range(1, batch)]
+    for source in first:
         block_arrival(source).wait_recv()
-        return take(source, totals)
-
-    totals = lax.fori_loop(1, n, take_arrival, totals)
+    totals = take([me] + first, totals)
+
+    def take_batch(g, totals):
+        sources = [peer_at(g * batch + r) for r in range(batch)]
+        for source in sources:
+            block_arrival(source).wait_recv()
+        return take(sources, totals)
+
+    totals = lax.fori_loop(1, n // batch, take_batch, totals)
     composite = [total / total[bands:] for total in totals]
 
     def finish(source):
-        sums = part[source]
+        sums = early[source]
         for i in range(dates):
             sum_y = sum_xy = 0.0
             for t in range(mine):
@@ -128,17 +145,9 @@
                 sum_xy = sum_xy + fit_x * composite[t]
             sums = jnp.where(lane == 4 * i + 2, lane_sum(sum_y), sums)
             sums = jnp.where(lane == 4 * i + 3, lane_sum(sum_xy), sums)
-        part[source] = sums
-
-    def finish_peer(k, carry):
-        finish(lax.rem(me + k, n))
-        return carry
-
-    lax.fori_loop(0, n, finish_peer, 0, unroll=min(n, 16))
-    got[me] = part[me]
-
-    def sums_copy(k):
-        peer = lax.rem(me + k, n)
+        return sums
+
+    def sums_copy(peer):
         return pltpu.make_async_remote_copy(
             src_ref=part.at[peer],
             dst_ref=got.at[me],
@@ -147,14 +156,20 @@
             device_id={AXIS: peer},
         )
 
-    def send_sums(k, carry):
-        sums_copy(k).start()
-        return carry
-
-    lax.fori_loop(1, n, send_sums, 0)
-
-    def take_sums(k, total):
-        source = lax.rem(me - k + n, n)
+    group = 8 if n % 8 == 0 else 1
+    for top in range(n, 0, -group):
+        peers = [me if spot == 0 else peer_at(spot) for spot in range(top - 1, top - group - 1, -1)]
+        done = [finish(peer) for peer in peers]
+        if top == group:
+            sums = done.pop()
+            peers.pop()
+        for peer, value in zip(peers, done):
+            part[peer] = value
+        for peer in peers:
+            sums_copy(peer).start()
+
+    def take_sums(spot, total):
+        source = peer_at(spot)
         pltpu.make_async_remote_copy(
             src_ref=part.at[source],
             dst_ref=got.at[source],
@@ -164,26 +179,26 @@
         ).wait_recv()
         return total + got[source]
 
-    sums = lax.fori_loop(1, n, take_sums, got[me])
+    sums = lax.fori_loop(1, n, take_sums, sums)
+    weight_sum = sums[bands:, 0:1]
+    for i in range(1, dates):
+        weight_sum = jnp.where(lane >= 4 * i, sums[bands:, 4 * i:4 * i + 1], weight_sum)
+    mean_x = sums / weight_sum
+    mean_xx, mean_y, mean_xy = (pltpu.roll(mean_x, LANES - s, 1) for s in (1, 2, 3))
+    gains = (mean_xy - mean_x * mean_y) / (mean_xx - mean_x * mean_x + 1e-5)
+    offsets = mean_y - gains * mean_x
     for i in range(dates):
-        sum_x, sum_xx, sum_y, sum_xy = (sums[:, 4 * i + s:4 * i + s + 1] for s in range(4))
-        total = sum_x[bands:]
-        mean_x = sum_x / total
-        mean_y = sum_y / total
-        spread = sum_xx / total - mean_x * mean_x + 1e-5
-        gain = (sum_xy / total - mean_x * mean_y) / spread
-        offset = mean_y - gain * mean_x
-        gain = jnp.broadcast_to(gain, (rows, LANES))
-        offset = jnp.broadcast_to(offset, (rows, LANES))
+        gain = jnp.broadcast_to(gains[:, 4 * i:4 * i + 1], (rows, LANES))
+        offset = jnp.broadcast_to(offsets[:, 4 * i:4 * i + 1], (rows, LANES))
         for b in range(bands):
             for h in range(halves):
                 values = wide[i, h, b * tiles:(b + 1) * tiles]
                 scaled = gain[b:b + 1] * values + offset[b:b + 1]
                 out_ref[i, b, :, h * LANES:(h + 1) * LANES] = scaled.astype(out_ref.dtype)
 
-    def drain(k, carry):
-        block_copy(k).wait_send()
-        sums_copy(k).wait_send()
+    def drain(spot, carry):
+        block_copy(peer_at(spot)).wait_send()
+        sums_copy(peer_at(spot)).wait_send()
         return carry
 
     lax.fori_loop(1, n, drain, 0)
@@ -210,6 +225,7 @@
             pltpu.VMEM((n, mine, dates, rows, pix), jnp.float32),
             pltpu.VMEM((n, rows, LANES), jnp.float32),
             pltpu.VMEM((n, rows, LANES), jnp.float32),
+            pltpu.VMEM((n, rows, LANES), jnp.float32),
             pltpu.SemaphoreType.DMA((3,)),
             pltpu.SemaphoreType.DMA((n,)),
             pltpu.SemaphoreType.DMA((n,)),

time: 18.6 us -> 19.3 us (1.038)
  Pallas kernels: 17 us -> 17.7 us
    pallas_call x1, Pallas kernels: 17 us -> 17.7 us  [local(): pl.pallas_call(functools.partial(fused, n), out_shape=jax.ShapeDtypeStruc...]
where the time goes in v5:
time: 19.3 us; the launch traced here: 19.1 us
  Pallas kernels  17.7 us (92%)
  between operations  0.66 us (3%)
  local copies, waits for them, and re-layouts  0.65 us (3%)
    pallas_call x1, Pallas kernels, local(): pl.pallas_call(functools.partial(fused, n), out_shape=jax.ShapeDtypeStruc...  17.7 us
    unnamed x1, local copies, waits for them, and re-layouts  0.65 us

profile of v5, /device:TPU:0, one launch (start us, length us, event | category | flops | bytes accessed | tf_op | source)
XLA Modules:
  0.0 19.1 jit_solution(4110929809601124675)
XLA Ops:
  0.7 17.7 %shard_map.46 = bf16[2,7,16,256]{3,2,1,0:T(8,128)(2,1)S(1)} custom-call(bf16[2,7,16,256]{3,2,1,0:T(8,128)(2,1)} %bitcast.3, bf16[2,16,256]{2,1,0:T(8,128)(2,1)} %quality_hbm.1, f32[1,256]{1,0:T(1,128)} %mask_hbm.1, s32[1]{0:T(128)S(6)} %copy.6.counts_ref), custom_call_target="tpu_custom_call" | custom-call | tf_op jit(solution)/shard_map/pallas_call | solution.py:213
  18.4 0.6 %copy.7 = bf16[2,16,7,256]{3,1,2,0:T(8,128)(2,1)} copy(bf16[2,16,7,256]{3,1,2,0:T(8,128)(2,1)S(1)} %bitcast.2) | data formatting | bytes 229376

commit v6 on v5

--- a/solution.py
+++ b/solution.py
@@ -56,10 +56,10 @@
     pl.semaphore_wait(barrier, n - 1)
 
     def peer_at(spot):
-        step = spot - 1
-        half, odd = lax.div(step, 2), lax.rem(step, 2)
-        ahead = (1 + half) * (1 - odd) + (n - 1 - half) * odd
-        return lax.rem(me + ahead, n)
+        return lax.rem(me + spot, n)
+
+    def source_at(spot):
+        return lax.rem(me - spot + n, n)
 
     def block_copy(peer):
         return pltpu.make_async_remote_copy(
@@ -80,7 +80,7 @@
         )
 
     def send_block(k, carry):
-        block_copy(peer_at(n - k)).start()
+        block_copy(peer_at(k)).start()
         return carry
 
     lax.fori_loop(1, n, send_block, 0)
@@ -121,13 +121,13 @@
 
     batch = 4 if n % 4 == 0 else 1
     totals = tuple(jnp.zeros((rows, pix), jnp.float32) for _ in range(mine))
-    first = [peer_at(spot) for spot in range(1, batch)]
+    first = [source_at(spot) for spot in range(1, batch)]
     for source in first:
         block_arrival(source).wait_recv()
     totals = take([me] + first, totals)
 
     def take_batch(g, totals):
-        sources = [peer_at(g * batch + r) for r in range(batch)]
+        sources = [source_at(g * batch + r) for r in range(batch)]
         for source in sources:
             block_arrival(source).wait_recv()
         return take(sources, totals)
@@ -157,10 +157,10 @@
         )
 
     group = 8 if n % 8 == 0 else 1
-    for top in range(n, 0, -group):
-        peers = [me if spot == 0 else peer_at(spot) for spot in range(top - 1, top - group - 1, -1)]
+    for low in range(0, n, group):
+        peers = [peer_at(low + r + 1) for r in range(group)]
         done = [finish(peer) for peer in peers]
-        if top == group:
+        if low + group == n:
             sums = done.pop()
             peers.pop()
         for peer, value in zip(peers, done):
@@ -169,7 +169,7 @@
             sums_copy(peer).start()
 
     def take_sums(spot, total):
-        source = peer_at(spot)
+        source = source_at(spot)
         pltpu.make_async_remote_copy(
             src_ref=part.at[source],
             dst_ref=got.at[source],

time: 19.3 us -> 18.4 us (0.953)
  Pallas kernels: 17.7 us -> 16.9 us
    pallas_call x1, Pallas kernels: 17.7 us -> 16.9 us  [local(): pl.pallas_call(functools.partial(fused, n), out_shape=jax.ShapeDtypeStruc...]
where the time goes in v6:
time: 18.4 us; the launch traced here: 18.2 us
  Pallas kernels  16.9 us (92%)
  between operations  0.66 us (4%)
  local copies, waits for them, and re-layouts  0.65 us (4%)
    pallas_call x1, Pallas kernels, local(): pl.pallas_call(functools.partial(fused, n), out_shape=jax.ShapeDtypeStruc...  16.9 us
    unnamed x1, local copies, waits for them, and re-layouts  0.65 us

profile of v6, /device:TPU:0, one launch (start us, length us, event | category | flops | bytes accessed | tf_op | source)
XLA Modules:
  0.0 18.2 jit_solution(4529662687238770096)
XLA Ops:
  0.7 16.9 %shard_map.46 = bf16[2,7,16,256]{3,2,1,0:T(8,128)(2,1)S(1)} custom-call(bf16[2,7,16,256]{3,2,1,0:T(8,128)(2,1)} %bitcast.3, bf16[2,16,256]{2,1,0:T(8,128)(2,1)} %quality_hbm.1, f32[1,256]{1,0:T(1,128)} %mask_hbm.1, s32[1]{0:T(128)S(6)} %copy.6.counts_ref), custom_call_target="tpu_custom_call" | custom-call | tf_op jit(solution)/shard_map/pallas_call | solution.py:213
  17.5 0.6 %copy.7 = bf16[2,16,7,256]{3,1,2,0:T(8,128)(2,1)} copy(bf16[2,16,7,256]{3,1,2,0:T(8,128)(2,1)S(1)} %bitcast.2) | data formatting | bytes 229376

commit v7 on v6

--- a/solution.py
+++ b/solution.py
@@ -87,6 +87,9 @@
 
     last_row = lax.broadcasted_iota(jnp.int32, (rows, pix), 0) == bands
     lane = lax.broadcasted_iota(jnp.int32, (rows, LANES), 1)
+    width = 4 * dates
+    base = width * bands
+    slot = lane + width * lax.broadcasted_iota(jnp.int32, (rows, LANES), 0) - base
 
     def lane_sum(values):
         return jnp.sum(values, axis=1, keepdims=True)
@@ -110,8 +113,8 @@
                     parts.append((t, i, fit_x))
                     sum_x = sum_x + fit_x
                     sum_xx = sum_xx + fit_x * values
-                sums = jnp.where(lane == 4 * i, lane_sum(sum_x), sums)
-                sums = jnp.where(lane == 4 * i + 1, lane_sum(sum_xx), sums)
+                sums = jnp.where(slot == 4 * i, lane_sum(sum_x), sums)
+                sums = jnp.where(slot == 4 * i + 1, lane_sum(sum_xx), sums)
             kept.append((source, sums, parts))
         for source, sums, parts in kept:
             early[source] = sums
@@ -143,9 +146,9 @@
                 fit_x = fitted[source, t, i]
                 sum_y = sum_y + fit_x[bands:] * composite[t]
                 sum_xy = sum_xy + fit_x * composite[t]
-            sums = jnp.where(lane == 4 * i + 2, lane_sum(sum_y), sums)
-            sums = jnp.where(lane == 4 * i + 3, lane_sum(sum_xy), sums)
-        return sums
+            sums = jnp.where(slot == 4 * i + 2, lane_sum(sum_y), sums)
+            sums = jnp.where(slot == 4 * i + 3, lane_sum(sum_xy), sums)
+        return jnp.sum(sums, axis=0, keepdims=True)
 
     def sums_copy(peer):
         return pltpu.make_async_remote_copy(
@@ -180,16 +183,18 @@
         return total + got[source]
 
     sums = lax.fori_loop(1, n, take_sums, sums)
-    weight_sum = sums[bands:, 0:1]
+    sums = jnp.broadcast_to(sums, (rows, LANES))
+    sums = pltpu.roll(sums, 0, 1, stride=width, stride_axis=0)
+    weight_sum = sums[bands:, base:base + 1]
     for i in range(1, dates):
-        weight_sum = jnp.where(lane >= 4 * i, sums[bands:, 4 * i:4 * i + 1], weight_sum)
+        weight_sum = jnp.where(lane >= base + 4 * i, sums[bands:, base + 4 * i:base + 4 * i + 1], weight_sum)
     mean_x = sums / weight_sum
     mean_xx, mean_y, mean_xy = (pltpu.roll(mean_x, LANES - s, 1) for s in (1, 2, 3))
     gains = (mean_xy - mean_x * mean_y) / (mean_xx - mean_x * mean_x + 1e-5)
     offsets = mean_y - gains * mean_x
     for i in range(dates):
-        gain = jnp.broadcast_to(gains[:, 4 * i:4 * i + 1], (rows, LANES))
-        offset = jnp.broadcast_to(offsets[:, 4 * i:4 * i + 1], (rows, LANES))
+        gain = jnp.broadcast_to(gains[:, base + 4 * i:base + 4 * i + 1], (rows, LANES))
+        offset = jnp.broadcast_to(offsets[:, base + 4 * i:base + 4 * i + 1], (rows, LANES))
         for b in range(bands):
             for h in range(halves):
                 values = wide[i, h, b * tiles:(b + 1) * tiles]
@@ -224,8 +229,8 @@
             pltpu.VMEM((n, mine, dates, rows, pix), scenes.dtype),
             pltpu.VMEM((n, mine, dates, rows, pix), jnp.float32),
             pltpu.VMEM((n, rows, LANES), jnp.float32),
-            pltpu.VMEM((n, rows, LANES), jnp.float32),
-            pltpu.VMEM((n, rows, LANES), jnp.float32),
+            pltpu.VMEM((n, 1, LANES), jnp.float32),
+            pltpu.VMEM((n, 1, LANES), jnp.float32),
             pltpu.SemaphoreType.DMA((3,)),
             pltpu.SemaphoreType.DMA((n,)),
             pltpu.SemaphoreType.DMA((n,)),

time: 18.4 us -> 18.4 us (level)
  no operation moved by 1% of the time
where the time goes in v7:
time: 18.4 us; the launch traced here: 18.1 us
  Pallas kernels  16.8 us (91%)
  between operations  0.66 us (4%)
  local copies, waits for them, and re-layouts  0.65 us (4%)
    pallas_call x1, Pallas kernels, local(): pl.pallas_call(functools.partial(fused, n), out_shape=jax.ShapeDtypeStruc...  16.8 us
    unnamed x1, local copies, waits for them, and re-layouts  0.65 us

profile of v7, /device:TPU:0, one launch (start us, length us, event | category | flops | bytes accessed | tf_op | source)
XLA Modules:
  0.0 18.1 jit_solution(17361794379496514886)
XLA Ops:
  0.7 16.8 %shard_map.46 = bf16[2,7,16,256]{3,2,1,0:T(8,128)(2,1)S(1)} custom-call(bf16[2,7,16,256]{3,2,1,0:T(8,128)(2,1)} %bitcast.3, bf16[2,16,256]{2,1,0:T(8,128)(2,1)} %quality_hbm.1, f32[1,256]{1,0:T(1,128)} %mask_hbm.1, s32[1]{0:T(128)S(6)} %copy.6.counts_ref), custom_call_target="tpu_custom_call" | custom-call | tf_op jit(solution)/shard_map/pallas_call | solution.py:218
  17.5 0.6 %copy.7 = bf16[2,16,7,256]{3,1,2,0:T(8,128)(2,1)} copy(bf16[2,16,7,256]{3,1,2,0:T(8,128)(2,1)S(1)} %bitcast.2) | data formatting | bytes 229376
